TPU v7x, 256 devices: a whole 4x4x8 slice. The times are simulated.
256 devices in a mesh: roll: 8 (over z), fsdp: 32 (over y, x, core).
Axes of the slice: x: 4, y: 4, z: 8, core: 2. Of those that a mesh axis runs over, the one named last changes fastest.
Arguments:
- hidden: bfloat16 [32768, 4096], P(('roll', 'fsdp')), may hold values from -24 to 24
- send_counts: int32 [32, 8, 8], P('fsdp'), may hold values from 8 to 24, as said below
- queries: bfloat16 [32768, 4096], P(('roll', 'fsdp')), may hold values from -90 to 90
- upstream: bfloat16 [32768, 4096], P(('roll', 'fsdp')), may hold values from -6 to 6
- norm_gain: float32 [4096], replicated, may hold values from 0.5 to 1.5
- kv_weight: bfloat16 [4096, 1024], P('fsdp'), may hold values from -0.09375 to 0.09375
- logp_new: float32 [256, 128], P(('roll', 'fsdp')), may hold values from -3 to 0
- logp_old: float32 [256, 128], P(('roll', 'fsdp')), may hold values from -3 to 0
- advantage: float32 [256, 4], P(('roll', 'fsdp')), may hold values from -4 to 4
- segment_ids: int32 [256, 128], P(('roll', 'fsdp')), may hold values from 0 to 3, never falling along the last dimension, each value on 1 to 64 neighbouring positions
- trim_mask: int32 [256, 128], P(('roll', 'fsdp')), may hold values 0 or 1
Outputs:
- d_queries: bfloat16 [32768, 4096], P(('roll', 'fsdp'))
- d_hidden: bfloat16 [32768, 4096], P(('roll', 'fsdp'))
- kv_grad: float32 [4096, 1024], P('fsdp')
Inputs may be any that keep to these rules, and one draw needn't show every extreme that they name: For each fsdp index, every row and every column of send_counts sums to 128; a rollout shard's rows are ordered by the learner shard they go to.
All inputs are finite; a program needn't handle non-finite values. No bound on the sum of `trim_mask` on one device may be relied on, other than what follows from the above.
Results may differ from a plain program's by a relative error of at most 0.008.
The roundings to bfloat16 on the way count: a program that leaves them out, or rounds other values in their place, can miss the bound.
Values may be sent and summed in bfloat16 or wider, within the bound.
A program may use at most 128 MiB of HBM per device.

v0:
```python
import math

import jax
import jax.numpy as jnp
from jax import lax
from jax.sharding import PartitionSpec as P

KV = 4
HD = 128
GROUP = 8


ratio_cap = 2.0
norm_eps = 1e-06


def exclusive_starts(counts):
    return jnp.cumsum(counts) - counts


def pack_rows(source_rows, starts, slot_cap):
    slot_index = jnp.arange(slot_cap, dtype=jnp.int32)
    picks = jnp.minimum(starts[:, None] + slot_index[None, :], source_rows.shape[0] - 1)
    chosen = jnp.take(source_rows, picks.reshape(-1), axis=0)
    return chosen.reshape(starts.shape[0], slot_cap, source_rows.shape[1])


def unpack_rows(buffer, starts, tok_rows):
    peer_count, slot_cap, row_width = buffer.shape
    position = jnp.arange(tok_rows, dtype=jnp.int32)
    owner_shard = jnp.sum((position[:, None] >= starts[None, :]).astype(jnp.int32), axis=1) - 1
    slot_index = position - jnp.take(starts, owner_shard)
    flat_index = owner_shard * slot_cap + slot_index
    return jnp.take(buffer.reshape(peer_count * slot_cap, row_width), flat_index, axis=0)


def token_weight(logp_new, logp_old, advantage, segment_ids, trim_mask):
    clipped = jnp.minimum(jnp.exp(logp_new - logp_old), ratio_cap)
    response = jnp.arange(advantage.shape[1], dtype=jnp.int32)
    picked = jnp.sum(
        jnp.where(segment_ids[:, :, None] == response[None, None, :], advantage[:, None, :], 0.0),
        axis=2,
    )
    return trim_mask.astype(jnp.float32) * picked * clipped


def normalize(source_rows, norm_gain):
    values_f = source_rows.astype(jnp.float32)
    inv_rms = lax.rsqrt(jnp.mean(values_f * values_f, axis=1, keepdims=True) + norm_eps)
    unit_rows = values_f * inv_rms
    return ((unit_rows * norm_gain).astype(jnp.bfloat16), unit_rows, inv_rms)


def attend(queries, keys_values, upstream, coefficient, segment_rows):
    tok_rows = queries.shape[0]
    kv_width = KV * HD
    keys_block = keys_values[:, :kv_width].reshape(tok_rows, KV, HD)
    values_block = keys_values[:, kv_width:].reshape(tok_rows, KV, HD)
    query_heads = queries.reshape(tok_rows, KV, GROUP, HD)
    score_scale = 1.0 / math.sqrt(HD)
    scores = (
        jnp.einsum("ikgd,jkd->kgij", query_heads, keys_block, preferred_element_type=jnp.float32)
        * score_scale
    )
    position = jnp.arange(tok_rows, dtype=jnp.int32)
    allowed = (segment_rows[:, None] == segment_rows[None, :]) & (
        position[None, :] <= position[:, None]
    )
    scores = jnp.where(allowed[None, None], scores, -jnp.inf)
    row_max = jnp.max(scores, axis=3, keepdims=True)
    expo = jnp.exp(scores - row_max)
    probs = expo / jnp.sum(expo, axis=3, keepdims=True)
    probs_low = probs.astype(jnp.bfloat16)
    attended = jnp.einsum(
        "kgij,jkd->ikgd", probs_low, values_block, preferred_element_type=jnp.float32
    )
    d_out = (coefficient[:, None] * upstream.astype(jnp.float32)).astype(jnp.bfloat16)
    d_out = d_out.reshape(tok_rows, KV, GROUP, HD)
    row_delta = jnp.sum(d_out.astype(jnp.float32) * attended, axis=3)
    d_probs = jnp.einsum("ikgd,jkd->kgij", d_out, values_block, preferred_element_type=jnp.float32)
    d_scores = (
        probs * (d_probs - jnp.transpose(row_delta, (1, 2, 0))[..., None]) * score_scale
    ).astype(jnp.bfloat16)
    d_query = jnp.einsum("kgij,jkd->ikgd", d_scores, keys_block, preferred_element_type=jnp.float32)
    d_query = d_query.astype(jnp.bfloat16).reshape(tok_rows, -1)
    d_keys = jnp.einsum("kgij,ikgd->jkd", d_scores, query_heads, preferred_element_type=jnp.float32)
    d_values = jnp.einsum("kgij,ikgd->jkd", probs_low, d_out, preferred_element_type=jnp.float32)
    d_kv = jnp.concatenate(
        [d_keys.reshape(tok_rows, kv_width), d_values.reshape(tok_rows, kv_width)], axis=1
    )
    return (d_query, d_kv.astype(jnp.bfloat16))


def shards(
    hidden,
    send_counts,
    queries,
    upstream,
    norm_gain,
    kv_weight,
    logp_new,
    logp_old,
    advantage,
    segment_ids,
    trim_mask,
):
    tok_rows = hidden.shape[0]
    roll_size = lax.axis_size("roll")
    fsdp_size = lax.axis_size("fsdp")
    slot_cap = tok_rows // roll_size + tok_rows // (2 * roll_size)
    my_roll = lax.axis_index("roll")
    group_counts = send_counts[0]
    send_starts = exclusive_starts(jnp.take(group_counts, my_roll, axis=0))
    recv_starts = exclusive_starts(jnp.take(group_counts, my_roll, axis=1))
    full_weight = lax.all_gather(kv_weight, "fsdp", axis=0, tiled=True)
    coefficient = token_weight(logp_new, logp_old, advantage, segment_ids, trim_mask)[0]
    arrived = lax.all_to_all(
        pack_rows(hidden, send_starts, slot_cap), "roll", split_axis=0, concat_axis=0, tiled=True
    )
    relaid = unpack_rows(arrived, recv_starts, tok_rows)
    normed, unit_rows, inv_rms = normalize(relaid, norm_gain)
    keys_values = jnp.dot(normed, full_weight, preferred_element_type=jnp.float32).astype(
        jnp.bfloat16
    )
    d_queries, d_kv = attend(queries, keys_values, upstream, coefficient, segment_ids[0])
    d_normed = lax.dot_general(
        d_kv, full_weight, (((1,), (1,)), ((), ())), preferred_element_type=jnp.float32
    )
    d_unit = d_normed * norm_gain
    d_rows = (
        inv_rms * (d_unit - unit_rows * jnp.mean(d_unit * unit_rows, axis=1, keepdims=True))
    ).astype(jnp.bfloat16)
    returned = lax.all_to_all(
        pack_rows(d_rows, recv_starts, slot_cap), "roll", split_axis=0, concat_axis=0, tiled=True
    )
    d_hidden = unpack_rows(returned, send_starts, tok_rows)
    grad_scale = 1.0 / math.sqrt(tok_rows * roll_size * fsdp_size)
    share = lax.psum_scatter(
        lax.dot_general(normed, d_kv, (((0,), (0,)), ((), ())), preferred_element_type=jnp.float32),
        "fsdp",
        scatter_dimension=0,
        tiled=True,
    )
    summed = lax.psum(share, "roll")
    kv_grad = summed * grad_scale
    return (d_queries, d_hidden, kv_grad)


def solution(mesh):
    placed = (
        P(("roll", "fsdp"), None),
        P("fsdp", None, None),
        P(("roll", "fsdp"), None),
        P(("roll", "fsdp"), None),
        P(),
        P("fsdp", None),
        P(("roll", "fsdp"), None),
        P(("roll", "fsdp"), None),
        P(("roll", "fsdp"), None),
        P(("roll", "fsdp"), None),
        P(("roll", "fsdp"), None),
    )
    return jax.shard_map(
        shards,
        mesh=mesh,
        in_specs=placed,
        out_specs=(P(("roll", "fsdp"), None), P(("roll", "fsdp"), None), P("fsdp", None)),
        check_vma=False,
    )
```

profile of v0, /device:TPU:1, one launch (start us, length us, event | category | flops | bytes accessed | tf_op | source)
XLA Modules:
  0.0 296.6 jit_solution(8865534062139331596)
XLA Ops:
  13.2 9.2 %all-to-all-start = ((bf16[8,24,4096]{2,1,0:T(8,128)(2,1)}), bf16[8,24,4096]{2,1,0:T(8,128)(2,1)S(1)}, u32[]{:S(2)}, u32[]{:S(2)}) async-start(bf16[8,24,4096]{2,1,0:T(8,128)(2,1)} %bitcast.98), calls=%async_computation | async-start | bytes 3145728 | tf_op jit(solution)/shard_map/all_to_all | solution.py:117
  22.9 2.5 multiply_convert_fusion
  25.4 2.3 copy.29
  27.6 2.3 copy.59
  30.7 5.1 %compare_and_fusion.2 = (pred[128]{0:T(512)(128)(4,1)S(1)}, s32[128]{0:T(128)S(1)}) fusion(s32[]{:T(128)} %bitcast.8, s32[]{:T(128)} %bitcast.7, s32[]{:T(128)} %bitcast.6, s32[]{:T(128)} %bitcast.5, s32[]{:T(128)} %bitcast.4, s32[]{:T(128)} %bitcast.3, s32[]{:T(128)} %bitcast.2, s32[]{:T(128)} %bitcast.1, s32[128]{0:T(128)S(1)} %convert_reduce_fusion.1), kind=kLoop, calls=%fused_computation.77 | loop fusion | flops 3968 | bytes 1184 | tf_op jit(solution)/shard_map/jit(_take)/and | solution.py:34
  35.9 24.7 %all-to-all-done = bf16[8,24,4096]{2,1,0:T(8,128)(2,1)S(1)} async-done(((bf16[8,24,4096]{2,1,0:T(8,128)(2,1)}), bf16[8,24,4096]{2,1,0:T(8,128)(2,1)S(1)}, u32[]{:S(2)}, u32[]{:S(2)}) %all-to-all-start) | async-done | bytes 1572896 | tf_op jit(solution)/shard_map/all_to_all | solution.py:117
  60.6 2.2 gather_fusion.1
  64.5 8.2 %all-gather.2.cloned.1.call-done = bf16[4096,1024]{1,0:T(8,128)(2,1)} async-done(((bf16[128,1024]{1,0:T(8,128)(2,1)}), bf16[4096,1024]{1,0:T(8,128)(2,1)}) %all-gather.2.cloned.1.call-update) | async-done | bytes 8388624 | tf_op jit(solution)/shard_map/all_gather | solution.py:115
  72.7 5.0 %convolution_convert_fusion.1 = bf16[128,1024]{1,0:T(8,128)(2,1)S(1)} fusion(bf16[4096,1024]{1,0:T(8,128)(2,1)} %all-gather.2.cloned.1.call-done, f32[4096]{0:T(1024)S(1)} %copy-done.5, f32[128]{0:T(128)S(1)} %add_rsqrt_fusion, bf16[128,4096]{1,0:T(8,128)(2,1)} %gather_fusion.1, pred[128]{0:T(512)(128)(4,1)S(1)} %get-tuple-element.36), kind=kOutput, calls=%fused_computation.30 | convolution fusion | flops 1076494336 | bytes 9716352 | tf_op jit(solution)/shard_map/dot_general | solution.py:122
  78.8 2.7 fusion.43
  81.6 2.2 fusion.16
  87.2 8.2 %fusion.21 = f32[4096,1024]{1,0:T(8,128)} fusion(f32[4096]{0:T(1024)S(1)} %copy-done.5, f32[128]{0:T(128)S(1)} %copy-done.16, bf16[128,512]{0,1:T(8,128)(2,1)S(1)} %bitcast.108, bf16[128,512]{0,1:T(8,128)(2,1)S(1)} %bitcast.103, bf16[128,4096]{1,0:T(8,128)(2,1)S(1)} %copy-done.1, pred[128]{0:T(512)(128)(4,1)S(1)} %copy-done.12), kind=kOutput, calls=%fused_computation.42 | convolution fusion | flops 1076887552 | bytes 18104960 | tf_op jit(solution)/shard_map/dot_general | solution.py:139
  97.4 6.4 %fusion.5 = (f32[128]{0:T(128)S(1)}, f32[128,4096]{1,0:T(8,128)S(1)}) fusion(f32[128]{0:T(128)S(1)} %copy-done.17, bf16[128,4096]{1,0:T(8,128)(2,1)S(1)} %copy-done.1, pred[128]{0:T(512)(128)(4,1)S(1)} %copy-done.13, f32[4096]{0:T(1024)S(1)} %copy-done.5, bf16[4096,1024]{1,0:T(8,128)(2,1)} %all-gather.2.cloned.1.call-done, ...), kind=kOutput, calls=%fused_computation.12 | convolution fusion | flops 1077411712 | bytes 11814016 | tf_op jit(solution)/shard_map/dot_general | solution.py:126
  104.5 3.0 gather_fusion.2
  107.4 3.0 %broadcast_select_fusion = bf16[192,4096]{1,0:T(8,128)(2,1)} fusion(bf16[192,4096]{1,0:T(8,128)(2,1)} %gather_fusion.2, pred[192]{0:T(512)(128)(4,1)S(1)} %copy-done.24), kind=kLoop, calls=%fused_computation.27 | loop fusion | flops 786432 | bytes 3145920 | tf_op jit(solution)/shard_map/jit(_take)/select_n | solution.py:24
  110.4 6.8 %all-to-all-start.1 = ((bf16[8,24,4096]{2,1,0:T(8,128)(2,1)}), bf16[8,24,4096]{2,1,0:T(8,128)(2,1)S(1)}, u32[]{:S(2)}, u32[]{:S(2)}) async-start(bf16[8,24,4096]{2,1,0:T(8,128)(2,1)} %bitcast.99), calls=%async_computation.1 | async-start | bytes 3145728 | tf_op jit(solution)/shard_map/all_to_all | solution.py:133
  118.1 5.0 %compare_and_fusion = (pred[128]{0:T(512)(128)(4,1)S(1)}, s32[128]{0:T(128)S(1)}) fusion(s32[]{:T(128)} %bitcast.36, s32[]{:T(128)} %bitcast.35, s32[]{:T(128)} %bitcast.34, s32[]{:T(128)} %bitcast.33, s32[]{:T(128)} %bitcast.32, s32[]{:T(128)} %bitcast.31, s32[]{:T(128)} %bitcast.30, s32[]{:T(128)} %bitcast.29, s32[128]{0:T(128)S(1)} %convert_reduce_fusion), kind=kLoop, calls=%fused_computation.67 | loop fusion | flops 3968 | bytes 1184 | tf_op jit(solution)/shard_map/jit(_take)/and | solution.py:34
  123.1 2.7 convolution_convert_fusion
  125.9 2.3 copy.39
  128.2 27.3 %all-to-all-done.1 = bf16[8,24,4096]{2,1,0:T(8,128)(2,1)S(1)} async-done(((bf16[8,24,4096]{2,1,0:T(8,128)(2,1)}), bf16[8,24,4096]{2,1,0:T(8,128)(2,1)S(1)}, u32[]{:S(2)}, u32[]{:S(2)}) %all-to-all-start.1) | async-done | bytes 1572896 | tf_op jit(solution)/shard_map/all_to_all | solution.py:133
  155.5 2.2 gather_fusion.3
  157.7 58.7 %reduce-scatter.2.cloned.1.call-done = f32[128,1024]{1,0:T(8,128)} async-done(((f32[4096,1024]{1,0:T(8,128)}), f32[128,1024]{1,0:T(8,128)}) %reduce-scatter.2.cloned.1.call-update) | async-done | bytes 524304 | tf_op jit(solution)/shard_map/reduce_scatter | solution.py:138
  216.4 2.4 broadcast_select_fusion.2
  218.8 69.4 %all-reduce.2.cloned.1.call-done = f32[128,1024]{1,0:T(8,128)} async-done(((f32[128,1024]{1,0:T(8,128)}), f32[128,1024]{1,0:T(8,128)}) %all-reduce.2.cloned.1.call-update) | async-done | bytes 524304 | tf_op jit(solution)/shard_map/psum | solution.py:144
  (102 shorter events, 18.7 us)
Async XLA Ops:
  7.2 3.1 %copy-start = (bf16[128,4096]{1,0:T(8,128)(2,1)S(1)}, bf16[128,4096]{1,0:T(8,128)(2,1)}, u32[]{:S(2)}) copy-start(bf16[128,4096]{1,0:T(8,128)(2,1)} %param.17) | copy-start | bytes 3145732
  7.2 65.6 %all-gather.2.cloned.1.call-start = ((), (), s32[]{:S(2)}) async-start(), calls=%async_computation.3 | async-start | bytes 8650752 | tf_op jit(solution)/shard_map/all_gather | solution.py:115
  13.2 9.2 %copy-start.19 = (s32[1,8,8]{2,1,0:T(8,128)S(1)}, s32[1,8,8]{2,1,0:T(8,128)}, u32[]{:S(2)}) copy-start(s32[1,8,8]{2,1,0:T(8,128)} %param.18) | copy-start | bytes 772
  13.2 9.6 %copy-start.20 = (s32[1,128]{1,0:T(1,128)S(1)}, s32[1,128]{1,0:T(1,128)}, u32[]{:S(2)}) copy-start(s32[1,128]{1,0:T(1,128)} %param.26) | copy-start | bytes 1540
  13.2 9.6 %copy-start.25 = (f32[1,4]{1,0:T(1,128)S(1)}, f32[1,4]{1,0:T(1,128)}, u32[]{:S(2)}) copy-start(f32[1,4]{1,0:T(1,128)} %param.25) | copy-start | bytes 52
  13.2 9.7 %copy-start.21 = (f32[1,128]{1,0:T(1,128)S(1)}, f32[1,128]{1,0:T(1,128)}, u32[]{:S(2)}) copy-start(f32[1,128]{1,0:T(1,128)} %param.23) | copy-start | bytes 1540
  13.2 9.7 %copy-start.22 = (f32[1,128]{1,0:T(1,128)S(1)}, f32[1,128]{1,0:T(1,128)}, u32[]{:S(2)}) copy-start(f32[1,128]{1,0:T(1,128)} %param.24) | copy-start | bytes 1540
  13.2 9.7 %copy-start.23 = (s32[1,128]{1,0:T(1,128)S(1)}, s32[1,128]{1,0:T(1,128)}, u32[]{:S(2)}) copy-start(s32[1,128]{1,0:T(1,128)} %param.27) | copy-start | bytes 1540
  13.2 47.4 %all-to-all-start = ((bf16[8,24,4096]{2,1,0:T(8,128)(2,1)}), bf16[8,24,4096]{2,1,0:T(8,128)(2,1)S(1)}, u32[]{:S(2)}, u32[]{:S(2)}) async-start(bf16[8,24,4096]{2,1,0:T(8,128)(2,1)} %bitcast.98), calls=%async_computation | async-start | bytes 3145728 | tf_op jit(solution)/shard_map/all_to_all | solution.py:117
  22.3 194.0 %reduce-scatter.2.cloned.1.call-start = ((), (), s32[]{:S(2)}) async-start(), calls=%async_computation.4 | async-start | bytes 17301504 | tf_op jit(solution)/shard_map/reduce_scatter | solution.py:138
  29.9 5.9 %copy-start.9 = (s32[8]{0:T(128)}, s32[8]{0:T(128)S(1)}, u32[]{:S(2)}) copy-start(s32[8]{0:T(128)S(1)} %bitcast_subtract_fusion.2) | copy-start | bytes 100
  35.8 37.0 %copy-start.11 = (pred[128]{0:T(512)(128)(4,1)}, pred[128]{0:T(512)(128)(4,1)S(1)}, u32[]{:S(2)}) copy-start(pred[128]{0:T(512)(128)(4,1)S(1)} %get-tuple-element.36) | copy-start | bytes 388
  60.6 12.1 %copy-start.5 = (f32[4096]{0:T(1024)S(1)}, f32[4096]{0:T(1024)}, u32[]{:S(2)}) copy-start(f32[4096]{0:T(1024)} %param.21) | copy-start | bytes 49156
  64.5 13.3 %copy-start.15 = (f32[128]{0:T(128)}, f32[128]{0:T(128)S(1)}, u32[]{:S(2)}) copy-start(f32[128]{0:T(128)S(1)} %add_rsqrt_fusion) | copy-start | bytes 1540
  64.5 14.3 %copy-start.3 = (bf16[128,4096]{0,1:T(8,128)(2,1)S(1)}, bf16[128,4096]{0,1:T(8,128)(2,1)}, u32[]{:S(2)}) copy-start(bf16[128,4096]{0,1:T(8,128)(2,1)} %copy.59) | copy-start | bytes 3145732
  78.8 2.8 copy-start.4
  81.6 2.3 copy-start.26
  81.6 2.3 copy-start.27
  97.4 6.5 %copy-start.14 = (pred[128]{0:T(512)(128)(4,1)S(1)}, pred[128]{0:T(512)(128)(4,1)}, u32[]{:S(2)}) copy-start(pred[128]{0:T(512)(128)(4,1)} %copy-done.11) | copy-start | bytes 388
  97.4 6.5 %copy-start.18 = (f32[128]{0:T(128)S(1)}, f32[128]{0:T(128)}, u32[]{:S(2)}) copy-start(f32[128]{0:T(128)} %copy-done.15) | copy-start | bytes 1540
  104.5 3.0 copy-start.24
  110.4 6.9 %copy-start.8 = (s32[8]{0:T(128)S(1)}, s32[8]{0:T(128)}, u32[]{:S(2)}) copy-start(s32[8]{0:T(128)} %copy-done.7) | copy-start | bytes 100
  110.4 45.1 %all-to-all-start.1 = ((bf16[8,24,4096]{2,1,0:T(8,128)(2,1)}), bf16[8,24,4096]{2,1,0:T(8,128)(2,1)S(1)}, u32[]{:S(2)}, u32[]{:S(2)}) async-start(bf16[8,24,4096]{2,1,0:T(8,128)(2,1)} %bitcast.99), calls=%async_computation.1 | async-start | bytes 3145728 | tf_op jit(solution)/shard_map/all_to_all | solution.py:133
  117.3 171.0 %all-reduce.2.cloned.1.call-start = ((), (), s32[]{:S(2)}) async-start(), calls=%async_computation.5 | async-start | bytes 1048576 | tf_op jit(solution)/shard_map/psum | solution.py:144
  (9 other events, 12.1 us)
Sparse Core Ops, SparseCore 0:
  10.6 62.1 all-gather.1
  95.6 120.7 reduce-scatter.1
  218.7 69.4 all-reduce.1
where the time goes:
time: 301 us; the launch traced here: 297 us
  waiting for transfers between devices  189 us (63%)
  matrix products  28.9 us (10%)
  other arithmetic  27.1 us (9%)
  local copies, waits for them, and re-layouts  21.4 us (7%)
  starting transfers between devices  16.1 us (5%)
  between operations  14.1 us (5%)
    psum x1, waiting for transfers between devices, shards(): summed = lax.psum(share, 'roll')  69.4 us
    reduce_scatter x1, waiting for transfers between devices, shards(): lax.psum_scatter(lax.dot_general(normed, d_kv, (((0,), (0,)), ((), ())),...  58.7 us
    all_to_all x1, waiting for transfers between devices, shards(): lax.all_to_all(pack_rows(d_rows, recv_starts, slot_cap), 'roll', split_ax...  27.3 us
    all_to_all x1, waiting for transfers between devices, shards(): lax.all_to_all(pack_rows(hidden, send_starts, slot_cap), 'roll', split_ax...  24.7 us
    and x2, other arithmetic, unpack_rows(): jnp.take(buffer.reshape(peer_count * slot_cap, row_width), flat_index, ax...  10.1 us
    all_to_all x1, starting transfers between devices, shards(): lax.all_to_all(pack_rows(hidden, send_starts, slot_cap), 'roll', split_ax...  9.16 us
    all_gather x1, waiting for transfers between devices, shards(): full_weight = lax.all_gather(kv_weight, 'fsdp', axis=0, tiled=True)  8.23 us
    dot_general x1, matrix products, shards(): lax.dot_general(normed, d_kv, (((0,), (0,)), ((), ())), preferred_element...  8.2 us
  transfers between devices with their start and end apart: 5, of which 5 were waited for; matrix products, arithmetic and copies ran while one was open for 17% of the time, Pallas kernels for 0%

commit v1 on v0

--- a/solution.py
+++ b/solution.py
@@ -114,35 +114,40 @@
     recv_starts = exclusive_starts(jnp.take(group_counts, my_roll, axis=1))
     full_weight = lax.all_gather(kv_weight, "fsdp", axis=0, tiled=True)
     coefficient = token_weight(logp_new, logp_old, advantage, segment_ids, trim_mask)[0]
-    arrived = lax.all_to_all(
-        pack_rows(hidden, send_starts, slot_cap), "roll", split_axis=0, concat_axis=0, tiled=True
-    )
-    relaid = unpack_rows(arrived, recv_starts, tok_rows)
-    normed, unit_rows, inv_rms = normalize(relaid, norm_gain)
-    keys_values = jnp.dot(normed, full_weight, preferred_element_type=jnp.float32).astype(
+    normed, unit_rows, inv_rms = normalize(hidden, norm_gain)
+    normed_columns = lax.all_to_all(
+        normed.reshape(tok_rows, fsdp_size, -1), "fsdp", split_axis=1, concat_axis=0, tiled=True
+    ).reshape(tok_rows * fsdp_size, -1)
+    projected = jnp.dot(normed, full_weight, preferred_element_type=jnp.float32).astype(
         jnp.bfloat16
     )
+    arrived = lax.all_to_all(
+        pack_rows(projected, send_starts, slot_cap), "roll", split_axis=0, concat_axis=0, tiled=True
+    )
+    keys_values = unpack_rows(arrived, recv_starts, tok_rows)
     d_queries, d_kv = attend(queries, keys_values, upstream, coefficient, segment_ids[0])
+    returned = lax.all_to_all(
+        pack_rows(d_kv, recv_starts, slot_cap), "roll", split_axis=0, concat_axis=0, tiled=True
+    )
+    d_projected = unpack_rows(returned, send_starts, tok_rows)
+    plane_d = lax.all_gather(d_projected, "fsdp", axis=0, tiled=True)
     d_normed = lax.dot_general(
-        d_kv, full_weight, (((1,), (1,)), ((), ())), preferred_element_type=jnp.float32
+        d_projected, full_weight, (((1,), (1,)), ((), ())), preferred_element_type=jnp.float32
     )
     d_unit = d_normed * norm_gain
-    d_rows = (
+    d_hidden = (
         inv_rms * (d_unit - unit_rows * jnp.mean(d_unit * unit_rows, axis=1, keepdims=True))
     ).astype(jnp.bfloat16)
-    returned = lax.all_to_all(
-        pack_rows(d_rows, recv_starts, slot_cap), "roll", split_axis=0, concat_axis=0, tiled=True
+    grad_scale = 1.0 / math.sqrt(tok_rows * roll_size * fsdp_size)
+    share = lax.dot_general(
+        normed_columns, plane_d, (((0,), (0,)), ((), ())), preferred_element_type=jnp.float32
     )
-    d_hidden = unpack_rows(returned, send_starts, tok_rows)
-    grad_scale = 1.0 / math.sqrt(tok_rows * roll_size * fsdp_size)
-    share = lax.psum_scatter(
-        lax.dot_general(normed, d_kv, (((0,), (0,)), ((), ())), preferred_element_type=jnp.float32),
-        "fsdp",
-        scatter_dimension=0,
-        tiled=True,
+    pieces = lax.all_to_all(
+        share.reshape(roll_size, -1, share.shape[1]), "roll", split_axis=0, concat_axis=0, tiled=True
     )
-    summed = lax.psum(share, "roll")
-    kv_grad = summed * grad_scale
+    kv_grad = lax.all_gather(
+        jnp.sum(pieces, axis=0) * grad_scale, "roll", axis=0, tiled=True
+    )
     return (d_queries, d_hidden, kv_grad)
 
 

time: 301 us -> 260 us (0.86)
  the two profiles are of different devices: /device:TPU:1 before, /device:TPU:2 now
where the time goes in v1:
time: 260 us; the launch traced here: 259 us
  waiting for transfers between devices  110 us (42%)
  blocking collectives  48.2 us (19%)
  other arithmetic  27.2 us (10%)
  matrix products  26 us (10%)
  starting transfers between devices  19.3 us (7%)
  between operations  14.3 us (6%)
  local copies, waits for them, and re-layouts  14.1 us (5%)
    all_gather x1, waiting for transfers between devices, shards(): full_weight = lax.all_gather(kv_weight, 'fsdp', axis=0, tiled=True)  54.3 us
    all_gather x1, waiting for transfers between devices, shards(): plane_d = lax.all_gather(d_projected, 'fsdp', axis=0, tiled=True)  27.8 us
    all_gather x1, blocking collectives, shards(): lax.all_gather(jnp.sum(pieces, axis=0) * grad_scale, 'roll', axis=0, tile...  25.5 us
    all_to_all x1, blocking collectives, shards(): lax.all_to_all(normed.reshape(tok_rows, fsdp_size, -1), 'fsdp', split_axi...  22.8 us
    all_to_all x1, waiting for transfers between devices, shards(): lax.all_to_all(share.reshape(roll_size, -1, share.shape[1]), 'roll', spli...  16.2 us
    and x2, other arithmetic, unpack_rows(): jnp.take(buffer.reshape(peer_count * slot_cap, row_width), flat_index, ax...  10.5 us
    all_to_all x1, waiting for transfers between devices, shards(): lax.all_to_all(pack_rows(d_kv, recv_starts, slot_cap), 'roll', split_axis...  8.86 us
    all_to_all x1, starting transfers between devices, shards(): lax.all_to_all(share.reshape(roll_size, -1, share.shape[1]), 'roll', spli...  7.01 us
  transfers between devices with their start and end apart: 5, of which 5 were waited for; matrix products, arithmetic and copies ran while one was open for 15% of the time, Pallas kernels for 0%

profile of v1, /device:TPU:2, one launch (start us, length us, event | category | flops | bytes accessed | tf_op | source)
XLA Modules:
  0.0 259.1 jit_solution(7549491258751075687)
XLA Ops:
  12.9 1.5 fusion.11
  15.7 1.5 multiply_convert_fusion
  17.2 54.3 %all-gather.3.cloned.1.call-done = bf16[4096,1024]{1,0:T(8,128)(2,1)} async-done(((bf16[128,1024]{1,0:T(8,128)(2,1)}), bf16[4096,1024]{1,0:T(8,128)(2,1)}) %all-gather.3.cloned.1.call-update) | async-done | bytes 8388624 | tf_op jit(solution)/shard_map/all_gather | solution.py:115
  71.5 4.7 %convolution_convert_fusion.1 = bf16[128,1024]{1,0:T(8,128)(2,1)S(1)} fusion(bf16[4096,1024]{1,0:T(8,128)(2,1)} %all-gather.3.cloned.1.call-done, bf16[128,4096]{1,0:T(8,128)(2,1)S(1)} %copy-done, f32[4096]{0:T(1024)S(1)} %copy-done.4, f32[128]{0:T(128)S(1)} %add_rsqrt_fusion), kind=kOutput, calls=%fused_computation.30 | convolution fusion | flops 1075970048 | bytes 9716224 | tf_op jit(solution)/shard_map/dot_general | solution.py:121
  78.0 7.0 %all-to-all-start = ((bf16[8,24,1024]{2,1,0:T(8,128)(2,1)}), bf16[8,24,1024]{2,1,0:T(8,128)(2,1)S(1)}, u32[]{:S(2)}, u32[]{:S(2)}) async-start(bf16[8,24,1024]{2,1,0:T(8,128)(2,1)} %bitcast.12), calls=%async_computation | async-start | bytes 786432 | tf_op jit(solution)/shard_map/all_to_all | solution.py:124
  85.0 5.5 %compare_and_fusion.2 = (pred[128]{0:T(512)(128)(4,1)}, s32[128]{0:T(128)}) fusion(s32[]{:T(128)} %bitcast.8, s32[]{:T(128)} %bitcast.7, s32[]{:T(128)} %bitcast.6, s32[]{:T(128)} %bitcast.5, s32[]{:T(128)} %bitcast.4, s32[]{:T(128)} %bitcast.3, s32[]{:T(128)} %bitcast.2, s32[]{:T(128)} %bitcast.1, s32[128]{0:T(128)S(1)} %convert_reduce_fusion.1), kind=kLoop, calls=%fused_computation.80 | loop fusion | flops 3968 | bytes 1184 | tf_op jit(solution)/shard_map/jit(_take)/and | solution.py:34
  90.6 1.6 copy.76
  96.6 1.4 fusion.27
  98.0 2.1 all-to-all-done
  101.3 3.0 %fusion.42 = (f32[4,8,128]{2,1,0:T(8,128)S(1)}, f32[4,8,128,128]{2,3,1,0:T(8,128)}) fusion(pred[128,128]{0,1:T(8,128)(4,1)} %fusion.27, bf16[128,4,128,1]{0,2,3,1:T(8,128)(2,1)S(1)} %bitcast.137, bf16[128,4,8,128]{0,3,2,1:T(8,128)(2,1)S(1)} %bitcast.129), kind=kOutput, calls=%fused_computation.108 | convolution fusion | flops 136315008 | bytes 3309568 | tf_op jit(solution)/shard_map/sub | solution.py:71
  104.3 2.7 %fusion.18 = bf16[4,128,128]{2,1,0:T(8,128)(2,1)} fusion(bf16[128,4,8,128]{0,3,2,1:T(8,128)(2,1)S(1)} %bitcast.134, f32[4,8,128,128]{2,3,1,0:T(8,128)} %get-tuple-element.62, f32[4,8,128]{2,1,0:T(8,128)S(1)} %get-tuple-element.61), kind=kOutput, calls=%fused_computation.34 | convolution fusion | flops 135331840 | bytes 3293184 | tf_op jit(solution)/shard_map/kgij,ikgd->jkd/dot_general | solution.py:87
  108.8 2.2 fusion.12
  114.7 5.2 %all-to-all-start.1 = ((bf16[8,24,1024]{2,1,0:T(8,128)(2,1)}), bf16[8,24,1024]{2,1,0:T(8,128)(2,1)S(1)}, u32[]{:S(2)}, u32[]{:S(2)}) async-start(bf16[8,24,1024]{2,1,0:T(8,128)(2,1)} %bitcast.49), calls=%async_computation.1 | async-start | bytes 786432 | tf_op jit(solution)/shard_map/all_to_all | solution.py:129
  120.6 4.9 %compare_and_fusion = (pred[128]{0:T(512)(128)(4,1)S(1)}, s32[128]{0:T(128)S(1)}) fusion(s32[]{:T(128)} %bitcast.40, s32[]{:T(128)} %bitcast.39, s32[]{:T(128)} %bitcast.38, s32[]{:T(128)} %bitcast.37, s32[]{:T(128)} %bitcast.36, s32[]{:T(128)} %bitcast.35, s32[]{:T(128)} %bitcast.34, s32[]{:T(128)} %bitcast.33, s32[128]{0:T(128)S(1)} %convert_reduce_fusion), kind=kLoop, calls=%fused_computation.70 | loop fusion | flops 3968 | bytes 1184 | tf_op jit(solution)/shard_map/jit(_take)/and | solution.py:34
  125.6 8.9 %all-to-all-done.1 = bf16[8,24,1024]{2,1,0:T(8,128)(2,1)S(1)} async-done(((bf16[8,24,1024]{2,1,0:T(8,128)(2,1)}), bf16[8,24,1024]{2,1,0:T(8,128)(2,1)S(1)}, u32[]{:S(2)}, u32[]{:S(2)}) %all-to-all-start.1) | async-done | bytes 393248 | tf_op jit(solution)/shard_map/all_to_all | solution.py:129
  136.1 6.5 %fusion.7 = (f32[128]{0:T(128)S(1)}, f32[128,4096]{1,0:T(8,128)S(1)}) fusion(bf16[128,4096]{1,0:T(8,128)(2,1)S(1)} %copy-done, f32[128]{0:T(128)S(1)} %copy-done.9, f32[4096]{0:T(1024)S(1)} %copy-done.4, bf16[128,1024]{1,0:T(8,128)(2,1)} %broadcast_select_fusion.2, bf16[4096,1024]{1,0:T(8,128)(2,1)} %all-gather.3.cloned.1.call-done), kind=kOutput, calls=%fused_computation.14 | convolution fusion | flops 1076363136 | bytes 11813888 | tf_op jit(solution)/shard_map/dot_general | solution.py:134
  142.6 1.6 fusion.23
  144.5 22.8 %all_to_all.30 = bf16[128,32,128]{2,0,1:T(8,128)(2,1)S(1)} all-to-all(bf16[128,32,128]{2,0,1:T(8,128)(2,1)S(1)} %bitcast.132), channel_id=1, replica_groups=mesh['roll'=8,'fsdp'=32] {'fsdp'}, dimensions={1} | all-to-all | bytes 2097152 | tf_op jit(solution)/shard_map/all_to_all | solution.py:118
  167.8 27.8 %all-gather.5.cloned.1.call-done = bf16[4096,1024]{1,0:T(8,128)(2,1)} async-done(((bf16[128,1024]{1,0:T(8,128)(2,1)}), bf16[4096,1024]{1,0:T(8,128)(2,1)}) %all-gather.5.cloned.1.call-update) | async-done | bytes 8388624 | tf_op jit(solution)/shard_map/all_gather | solution.py:133
  195.6 5.4 %fusion.1 = f32[8,16,1024]{2,1,0:T(8,128)} fusion(bf16[8,16,4096]{2,1,0:T(8,128)(2,1)S(1)} %bitcast.128, bf16[4096,1024]{1,0:T(8,128)(2,1)} %all-gather.5.cloned.1.call-done), kind=kOutput, calls=%fused_computation.5 | convolution fusion | flops 1073741824 | bytes 9961472 | tf_op jit(solution)/shard_map/dot_general | solution.py:142
  201.0 7.0 %all-to-all-start.3 = ((f32[8,16,1024]{2,1,0:T(8,128)}), f32[8,16,1024]{2,1,0:T(8,128)S(1)}, u32[]{:S(2)}, u32[]{:S(2)}) async-start(f32[8,16,1024]{2,1,0:T(8,128)} %fusion.1), calls=%async_computation.3 | async-start | bytes 1048576 | tf_op jit(solution)/shard_map/all_to_all | solution.py:145
  208.4 1.3 copy.60
  209.7 16.2 %all-to-all-done.3 = f32[8,16,1024]{2,1,0:T(8,128)S(1)} async-done(((f32[8,16,1024]{2,1,0:T(8,128)}), f32[8,16,1024]{2,1,0:T(8,128)S(1)}, u32[]{:S(2)}, u32[]{:S(2)}) %all-to-all-start.3) | async-done | bytes 524320 | tf_op jit(solution)/shard_map/all_to_all | solution.py:145
  226.0 25.5 %all_gather.11 = f32[128,1024]{1,0:T(8,128)S(1)} all-gather(f32[16,1024]{1,0:T(8,128)S(1)} %broadcast_multiply_fusion), channel_id=1, replica_groups=mesh['roll'=8,'fsdp'=32] {'roll'}, dimensions={0}, use_global_device_ids=true | all-gather | bytes 589824 | tf_op jit(solution)/shard_map/all_gather | solution.py:148
  (83 shorter events, 24.2 us)
Async XLA Ops:
  7.2 64.3 %copy-start = (bf16[128,4096]{1,0:T(8,128)(2,1)S(1)}, bf16[128,4096]{1,0:T(8,128)(2,1)}, u32[]{:S(2)}) copy-start(bf16[128,4096]{1,0:T(8,128)(2,1)} %param.17) | copy-start | bytes 3145732
  7.2 64.3 %copy-start.4 = (f32[4096]{0:T(1024)S(1)}, f32[4096]{0:T(1024)}, u32[]{:S(2)}) copy-start(f32[4096]{0:T(1024)} %param.21) | copy-start | bytes 49156
  7.2 64.3 %all-gather.3.cloned.1.call-start = ((), (), s32[]{:S(2)}) async-start(), calls=%async_computation.4 | async-start | bytes 8650752 | tf_op jit(solution)/shard_map/all_gather | solution.py:115
  10.6 0.5 copy-start.5
  11.4 64.8 %copy-start.7 = (s32[192]{0:T(256)}, s32[192]{0:T(256)S(1)}, u32[]{:S(2)}) copy-start(s32[192]{0:T(256)S(1)} %min.25) | copy-start | bytes 2308
  14.4 57.0 %copy-start.8 = (f32[128]{0:T(128)}, f32[128]{0:T(128)S(1)}, u32[]{:S(2)}) copy-start(f32[128]{0:T(128)S(1)} %add_rsqrt_fusion) | copy-start | bytes 1540
  78.0 22.1 %all-to-all-start = ((bf16[8,24,1024]{2,1,0:T(8,128)(2,1)}), bf16[8,24,1024]{2,1,0:T(8,128)(2,1)S(1)}, u32[]{:S(2)}, u32[]{:S(2)}) async-start(bf16[8,24,1024]{2,1,0:T(8,128)(2,1)} %bitcast.12), calls=%async_computation | async-start | bytes 786432 | tf_op jit(solution)/shard_map/all_to_all | solution.py:124
  93.5 7.5 %copy-start.10 = (pred[128]{0:T(512)(128)(4,1)S(1)}, pred[128]{0:T(512)(128)(4,1)}, u32[]{:S(2)}) copy-start(pred[128]{0:T(512)(128)(4,1)} %get-tuple-element.39) | copy-start | bytes 388
  101.3 3.0 %copy-start.1 = (bf16[128,4096]{0,1:T(8,128)(2,1)S(1)}, bf16[128,4096]{0,1:T(8,128)(2,1)}, u32[]{:S(2)}) copy-start(bf16[128,4096]{0,1:T(8,128)(2,1)} %copy.48) | copy-start | bytes 3145732
  104.3 2.7 %copy-start.13 = (f32[4,8,128]{2,1,0:T(8,128)}, f32[4,8,128]{2,1,0:T(8,128)S(1)}, u32[]{:S(2)}) copy-start(f32[4,8,128]{2,1,0:T(8,128)S(1)} %get-tuple-element.61) | copy-start | bytes 49156
  108.8 2.2 copy-start.2
  108.8 2.2 copy-start.3
  108.8 2.6 %copy-start.12 = (f32[4,8,128,128]{2,3,1,0:T(8,128)S(1)}, f32[4,8,128,128]{2,3,1,0:T(8,128)}, u32[]{:S(2)}) copy-start(f32[4,8,128,128]{2,3,1,0:T(8,128)} %get-tuple-element.62) | copy-start | bytes 6291460
  108.8 2.6 %copy-start.14 = (f32[4,8,128]{2,1,0:T(8,128)S(1)}, f32[4,8,128]{2,1,0:T(8,128)}, u32[]{:S(2)}) copy-start(f32[4,8,128]{2,1,0:T(8,128)} %copy-done.13) | copy-start | bytes 49156
  112.6 1.2 copy-start.11
  112.6 7.3 %copy-start.6 = (s32[8]{0:T(128)S(1)}, s32[8]{0:T(128)}, u32[]{:S(2)}) copy-start(s32[8]{0:T(128)} %copy-done.5) | copy-start | bytes 100
  114.7 21.5 %copy-start.9 = (f32[128]{0:T(128)S(1)}, f32[128]{0:T(128)}, u32[]{:S(2)}) copy-start(f32[128]{0:T(128)} %copy-done.8) | copy-start | bytes 1540
  114.7 19.8 %all-to-all-start.1 = ((bf16[8,24,1024]{2,1,0:T(8,128)(2,1)}), bf16[8,24,1024]{2,1,0:T(8,128)(2,1)S(1)}, u32[]{:S(2)}, u32[]{:S(2)}) async-start(bf16[8,24,1024]{2,1,0:T(8,128)(2,1)} %bitcast.49), calls=%async_computation.1 | async-start | bytes 786432 | tf_op jit(solution)/shard_map/all_to_all | solution.py:129
  119.9 75.7 %all-gather.5.cloned.1.call-start = ((), (), s32[]{:S(2)}) async-start(), calls=%async_computation.5 | async-start | bytes 8650752 | tf_op jit(solution)/shard_map/all_gather | solution.py:133
  201.0 24.9 %all-to-all-start.3 = ((f32[8,16,1024]{2,1,0:T(8,128)}), f32[8,16,1024]{2,1,0:T(8,128)S(1)}, u32[]{:S(2)}, u32[]{:S(2)}) async-start(f32[8,16,1024]{2,1,0:T(8,128)} %fusion.1), calls=%async_computation.3 | async-start | bytes 1048576 | tf_op jit(solution)/shard_map/all_to_all | solution.py:145
Sparse Core Ops, SparseCore 0:
  10.6 60.8 all-gather.2
  136.2 59.2 all-gather.4

commit v2 on v0

v2 whole, which is shorter than its diff:
```python
import functools
import math

import jax
import jax.numpy as jnp
from jax import lax
from jax.experimental import pallas as pl
from jax.experimental.pallas import tpu as pltpu
from jax.sharding import PartitionSpec as P

KV = 4
HD = 128
GROUP = 8
D = 4096
ROWS = 128
KVW = KV * HD
SIDE = 4
CHIPS = SIDE * SIDE
ROLL = 8
SLOT = 24
PACKED = ROLL * 2 * SLOT
CHIP_COLS = D // CHIPS
SLICE = 2 * ROWS // ROLL
CHUNKS = 1

ratio_cap = 2.0
norm_eps = 1e-06
MESH = pl.DeviceIdType.MESH
F32 = jnp.float32
BF16 = jnp.bfloat16


def dot(a, b, dims=((1,), (0,))):
    return lax.dot_general(a, b, (dims, ((), ())), preferred_element_type=F32)


class Gather:
    def __init__(self, buf, send_sem, recv_sem, x, y, core):
        self.buf, self.send_sem, self.recv_sem = buf, send_sem, recv_sem
        self.x, self.y, self.core = x, y, core
        self.started = []

    def at(self, half, du, dv):
        dx, dy = (du, dv) if half == 0 else (dv, du)
        chip = lax.rem(self.y + dy + SIDE, SIDE) * SIDE + lax.rem(self.x + dx + SIDE, SIDE)
        return chip * 2 + self.core, chip

    def view(self, half, du, dv, quarter):
        ref = self.buf.at[self.at(half, du, dv)[1], half]
        return ref if quarter is None else ref.at[pl.ds(quarter * (ROWS // 2), ROWS // 2)]

    def send(self, half, block, step, sem, quarter=None):
        n = len(self.started)
        ref = self.view(half, *block, quarter)
        copy = pltpu.make_async_remote_copy(
            src_ref=ref,
            dst_ref=ref,
            send_sem=self.send_sem.at[n],
            recv_sem=self.recv_sem.at[half, sem],
            device_id={"fsdp": self.at(half, *step)[0]},
            device_id_type=MESH,
        )
        copy.start()
        self.started.append(copy)

    def arrive(self, half, block, sem, quarter=None):
        ref = self.view(half, *block, quarter)
        pltpu.make_async_copy(ref, ref, self.recv_sem.at[half, sem]).wait()

    def own(self, half):
        self.send(half, (0, 0), (1, 0), 0)
        self.send(half, (0, 0), (-1, 0), 1)
        self.second(half, 0)

    def second(self, half, j):
        du = (0, -1, 1, 2)[j]
        self.send(half, (du, 0), (0, 1), 4 + 4 * j)
        self.send(half, (du, 0), (0, -1), 5 + 4 * j)

    def first_near(self, half):
        self.arrive(half, (-1, 0), 0)
        self.send(half, (-1, 0), (1, 0), 2, 0)
        self.second(half, 1)
        self.arrive(half, (1, 0), 1)
        self.send(half, (1, 0), (-1, 0), 3, 1)
        self.second(half, 2)

    def first_far(self, half):
        self.arrive(half, (2, 0), 2, 0)
        self.arrive(half, (2, 0), 3, 1)
        self.second(half, 3)

    def second_near(self, half, j):
        du = (0, -1, 1, 2)[j]
        self.arrive(half, (du, -1), 4 + 4 * j)
        self.send(half, (du, -1), (0, 1), 6 + 4 * j, 0)
        self.arrive(half, (du, 1), 5 + 4 * j)
        self.send(half, (du, 1), (0, -1), 7 + 4 * j, 1)

    def second_far(self, half, j):
        du = (0, -1, 1, 2)[j]
        self.arrive(half, (du, 2), 6 + 4 * j, 0)
        self.arrive(half, (du, 2), 7 + 4 * j, 1)

    def finish(self):
        for copy in self.started:
            copy.wait_send()


def starts_of(counts):
    total, out = jnp.int32(0), []
    for count in counts:
        out.append(total)
        total = total + count
    return out


def selection(counts, across):
    starts = starts_of(counts)
    shape = (1, PACKED) if across else (PACKED, 1)
    place = lax.broadcasted_iota(jnp.int32, shape, 1 if across else 0)
    target = jnp.full(shape, -1, jnp.int32)
    for s in range(ROLL):
        for half in range(2):
            first = (2 * s + half) * SLOT
            inside = (place >= first) & (place < first + counts[s])
            inside = inside & (place < first + SLOT)
            target = jnp.where(inside, place + (starts[s] + (half * ROWS - first)), target)
    full = (2 * ROWS, PACKED) if across else (PACKED, 2 * ROWS)
    row = lax.broadcasted_iota(jnp.int32, full, 0 if across else 1)
    return jnp.where(row == target, 1.0, 0.0).astype(BF16)


def column_of(row):
    return jnp.transpose(jnp.broadcast_to(row, (ROWS, ROWS)))


def body(
    hid, cnt, qry, ups, gain, wgt, lpn, lpo, adv, seg, trm,
    dq_out, dh_out, kg_out,
    hv, qv, uv, dqv, dhv, nb, dn, wbuf, wother, dbuf, ncols, acc, kvx, kvown, dkvown,
    pack_s, pack_r, unpack_s, unpack_r, pk, rv, pk2, rv2, inv, bias, coef, ps, rs, rd, og, kgv,
    local_sem, pair_send, pair_recv, w_send, w_recv, d_send, d_recv,
    n_send, n_recv, z_send, z_recv, b_send, b_recv, r_send, r_recv, o_send, o_recv,
):
    z = lax.axis_index("roll")
    f = lax.axis_index("fsdp")
    core = lax.rem(f, 2)
    other = 1 - core
    chip = f // 2
    x = lax.rem(chip, SIDE)
    y = chip // SIDE
    partner = chip * 2 + other

    barrier = pltpu.get_barrier_semaphore()
    pl.semaphore_signal(barrier, inc=1, device_id={"fsdp": partner}, device_id_type=MESH)
    for d in range(1, CHIPS):
        peer = lax.rem(chip + d, CHIPS) * 2 + core
        pl.semaphore_signal(barrier, inc=1, device_id={"fsdp": peer}, device_id_type=MESH)
    for d in range(1, ROLL):
        for who in (f, partner):
            pl.semaphore_signal(
                barrier, inc=1, device_id={"roll": lax.rem(z + d, ROLL), "fsdp": who}, device_id_type=MESH
            )

    def local(src, dst, n):
        copy = pltpu.make_async_copy(src, dst, local_sem.at[n])
        copy.start()
        return copy

    pair_copies = []

    def to_partner(src, dst, n):
        copy = pltpu.make_async_remote_copy(
            src_ref=src, dst_ref=dst, send_sem=pair_send.at[n], recv_sem=pair_recv.at[n],
            device_id={"fsdp": partner}, device_id_type=MESH,
        )
        copy.start()
        pair_copies.append(copy)

    def from_partner(dst, n):
        pltpu.make_async_copy(dst, dst, pair_recv.at[n]).wait()

    mine = pl.ds(pl.multiple_of(core * KVW, KVW), KVW)
    theirs = pl.ds(pl.multiple_of(other * KVW, KVW), KVW)
    w_copy = local(wgt.at[:, mine], wbuf.at[chip, core], 0)
    h_copy = local(hid, hv, 1)
    q_copy = local(qry, qv, 2)
    u_copy = local(ups, uv, 3)

    pl.semaphore_wait(barrier, 1 + (CHIPS - 1) + 2 * (ROLL - 1))

    to_partner(wgt.at[:, theirs], wbuf.at[chip, core], 0)
    w_copy.wait()
    gather = Gather(wbuf, w_send, w_recv, x, y, core)

    def by_owner(do):
        do(0)
        do(1)

    from_partner(wbuf.at[chip, other], 0)
    by_owner(gather.own)

    h_copy.wait()
    square = jnp.zeros((ROWS, HD), F32)
    for c in range(D // HD):
        part = hv[:, c * HD:(c + 1) * HD].astype(F32)
        square = square + part * part
    inv_rms = lax.rsqrt(jnp.sum(square, axis=1, keepdims=True) * (1.0 / D) + norm_eps)
    inv[...] = jnp.broadcast_to(inv_rms, (ROWS, HD))
    for c in range(CHIPS):
        cols = slice(c * CHIP_COLS, (c + 1) * CHIP_COLS)
        nb[core, :, cols] = (hv[:, cols].astype(F32) * inv_rms * gain[:, cols]).astype(BF16)
    to_partner(nb.at[core], nb.at[core], 1)

    gather.first_near(0)
    gather.first_near(1)

    n_copies = []
    for d in range(1, CHIPS):
        to = lax.rem(chip + d, CHIPS)
        copy = pltpu.make_async_remote_copy(
            src_ref=nb.at[core, :, pl.ds(pl.multiple_of(to * CHIP_COLS, CHIP_COLS), CHIP_COLS)],
            dst_ref=ncols.at[chip, core],
            send_sem=n_send.at[d], recv_sem=n_recv.at[d],
            device_id={"fsdp": to * 2 + core}, device_id_type=MESH,
        )
        n_copies.append(copy)

    send_counts = [cnt[0, z, l] for l in range(ROLL)]
    recv_counts = [cnt[0, s, z] for s in range(ROLL)]
    unpack_s[...] = selection(send_counts, True)
    unpack_r[...] = selection(recv_counts, True)
    pack_s[...] = selection(send_counts, False)
    pack_r[...] = selection(recv_counts, False)
    segment = seg[...]
    picked = jnp.zeros((1, ROWS), F32)
    for r in range(4):
        picked = picked + jnp.where(segment == r, adv[0, r], 0.0)
    weight = trm[...].astype(F32) * picked * jnp.minimum(jnp.exp(lpn[...] - lpo[...]), ratio_cap)
    coef[...] = column_of(weight)
    row = lax.broadcasted_iota(jnp.int32, (ROWS, ROWS), 0)
    col = lax.broadcasted_iota(jnp.int32, (ROWS, ROWS), 1)
    segment_f = segment.astype(F32)
    same = column_of(segment_f) == jnp.broadcast_to(segment_f, (ROWS, ROWS))
    bias[...] = jnp.where(same & (col <= row), 0.0, -jnp.inf)

    gather.second_near(0, 0)
    gather.second_near(1, 0)
    gather.first_far(0)
    gather.first_far(1)

    def project(c, first=False):
        cols = pl.ds(pl.multiple_of(c * CHIP_COLS, CHIP_COLS), CHIP_COLS)
        left = nb[:, :, cols].reshape(2 * ROWS, CHIP_COLS)
        term = dot(left, wbuf[c].reshape(2 * ROWS, KVW))
        if first:
            acc[...] = term
        else:
            acc[...] += term

    def chip_at(dx, dy):
        return lax.rem(y + dy + SIDE, SIDE) * SIDE + lax.rem(x + dx + SIDE, SIDE)

    from_partner(nb.at[other], 1)
    project(chip, True)
    for dx, dy in ((1, 0), (-1, 0), (0, 1), (0, -1)):
        project(chip_at(dx, dy))
    for j in (1, 2):
        gather.second_near(0, j)
        gather.second_near(1, j)
    for dx, dy in ((1, 1), (-1, 1), (1, -1), (-1, -1)):
        project(chip_at(dx, dy))
    gather.second_near(0, 3)
    gather.second_near(1, 3)
    gather.second_far(0, 0)
    gather.second_far(1, 0)
    for dx, dy in ((2, 0), (0, 2)):
        project(chip_at(dx, dy))
    for j in (1, 2):
        gather.second_far(0, j)
        gather.second_far(1, j)
    for dx, dy in ((2, 1), (2, -1), (1, 2), (-1, 2)):
        project(chip_at(dx, dy))
    gather.second_far(0, 3)
    gather.second_far(1, 3)
    project(chip_at(2, 2))

    for r in range(2):
        kvx[r] = acc[r * ROWS:(r + 1) * ROWS, :].astype(BF16)
    to_partner(kvx.at[other], kvown.at[core], 2)
    kvown[core] = kvx[core]
    to_partner(wbuf, wother, 3)
    for copy in n_copies:
        copy.start()
    n_own = local(
        nb.at[core, :, pl.ds(pl.multiple_of(chip * CHIP_COLS, CHIP_COLS), CHIP_COLS)],
        ncols.at[chip, core], 4,
    )
    from_partner(kvown.at[other], 2)

    def heads(ref, h):
        cols = slice(h * HD, (h + 1) * HD)
        return jnp.concatenate([ref[0, :, cols], ref[1, :, cols]], axis=0)

    z_copies = []

    def relay(out_buf, in_buf, send_sem, recv_sem, h):
        for d in range(1, ROLL):
            to = lax.rem(z + d, ROLL)
            copy = pltpu.make_async_remote_copy(
                src_ref=out_buf.at[h, to], dst_ref=in_buf.at[h, z],
                send_sem=send_sem.at[h, d], recv_sem=recv_sem.at[h, d],
                device_id={"roll": to}, device_id_type=MESH,
            )
            copy.start()
            z_copies.append(copy)
        in_buf[h, z] = out_buf[h, z]

    def relayed(in_buf, recv_sem, h):
        for d in range(1, ROLL):
            ref = in_buf.at[h, lax.rem(z + ROLL - d, ROLL)]
            pltpu.make_async_copy(ref, ref, recv_sem.at[h, d]).wait()

    for h in range(KV):
        packed = dot(pack_s[...], heads(kvown, h)).astype(BF16)
        pk[h] = packed.reshape(ROLL, 2 * SLOT, HD)
        relay(pk, rv, z_send, z_recv, h)

    q_copy.wait()
    u_copy.wait()
    scale = 1.0 / math.sqrt(HD)
    stacked = (GROUP, ROWS, ROWS)
    dq_copies = []
    for h in range(KV):
        relayed(rv, z_recv, h)
        kv = dot(unpack_r[...], rv[h].reshape(PACKED, HD)).astype(BF16)
        keys, values = kv[:ROWS], kv[ROWS:]
        base = h * GROUP * HD
        q = jnp.concatenate([qv[:, base + g * HD:base + (g + 1) * HD] for g in range(GROUP)], axis=0)
        d_out = jnp.concatenate(
            [
                (coef[...] * uv[:, base + g * HD:base + (g + 1) * HD].astype(F32)).astype(BF16)
                for g in range(GROUP)
            ],
            axis=0,
        )
        scores = dot(q, keys, ((1,), (1,))).reshape(stacked) * scale + bias[...][None]
        d_probs = dot(d_out, values, ((1,), (1,))).reshape(stacked)
        expo = jnp.exp(scores - jnp.max(scores, axis=2, keepdims=True))
        probs = expo * (1.0 / jnp.sum(expo, axis=2, keepdims=True))
        probs_low = probs.astype(BF16)
        row_delta = jnp.sum(probs_low.astype(F32) * d_probs, axis=2, keepdims=True)
        d_scores = (probs * (d_probs - row_delta) * scale).astype(BF16)
        d_scores = d_scores.reshape(GROUP * ROWS, ROWS)
        probs_low = probs_low.reshape(GROUP * ROWS, ROWS)
        d_keys = dot(d_scores, q, ((0,), (0,)))
        d_values = dot(probs_low, d_out, ((0,), (0,)))
        d_rows = jnp.concatenate([d_keys, d_values], axis=0).astype(BF16)
        pk2[h] = dot(pack_r[...], d_rows).astype(BF16).reshape(ROLL, 2 * SLOT, HD)
        relay(pk2, rv2, b_send, b_recv, h)
        d_q = dot(d_scores, keys).astype(BF16)
        for g in range(GROUP):
            dqv[:, base + g * HD:base + (g + 1) * HD] = d_q[g * ROWS:(g + 1) * ROWS]
        dq_copies.append(
            local(dqv.at[:, pl.ds(base, GROUP * HD)], dq_out.at[:, pl.ds(base, GROUP * HD)], 5 + h)
        )

    for d in range(1, CHIPS):
        ref = ncols.at[lax.rem(chip + CHIPS - d, CHIPS), core]
        pltpu.make_async_copy(ref, ref, n_recv.at[d]).wait()
    n_own.wait()
    to_partner(ncols.at[:, core], ncols.at[:, core], 4)

    for h in range(KV):
        relayed(rv2, b_recv, h)
        back = dot(unpack_s[...], rv2[h].reshape(PACKED, HD)).astype(BF16)
        cols = slice(h * HD, (h + 1) * HD)
        dkvown[0, :, cols] = back[:ROWS]
        dkvown[1, :, cols] = back[ROWS:]
    to_partner(dkvown.at[other], dbuf.at[chip, core], 5)
    dbuf[chip, core] = dkvown[core]
    from_partner(dbuf.at[chip, other], 5)
    back = Gather(dbuf, d_send, d_recv, x, y, core)
    by_owner(back.own)
    from_partner(ncols.at[:, other], 4)
    from_partner(wother, 3)

    moment = [jnp.zeros((ROWS, HD), F32)]

    def row_grad(c):
        cols = slice(c * CHIP_COLS, (c + 1) * CHIP_COLS)
        d_n = dot(dkvown[core], wbuf[c].reshape(2 * ROWS, KVW), ((1,), (1,)))
        d_n = d_n + dot(dkvown[other], wother[c].reshape(2 * ROWS, KVW), ((1,), (1,)))
        d_n = d_n * gain[:, cols]
        dn[:, cols] = d_n
        for i in range(CHIP_COLS // HD):
            lanes = slice(c * CHIP_COLS + i * HD, c * CHIP_COLS + (i + 1) * HD)
            unit = hv[:, lanes].astype(F32) * inv[...]
            moment[0] = moment[0] + d_n[:, i * HD:(i + 1) * HD] * unit

    def row_out():
        mean = jnp.sum(moment[0], axis=1, keepdims=True) * (1.0 / D)
        inv_rms = inv[:, :1]
        for c in range(CHIPS):
            cols = slice(c * CHIP_COLS, (c + 1) * CHIP_COLS)
            unit = hv[:, cols].astype(F32) * inv_rms
            dhv[:, cols] = (inv_rms * (dn[:, cols] - unit * mean)).astype(BF16)
        return local(dhv, dh_out, 9)

    def grad(c, first=False):
        left = ncols[c].reshape(2 * ROWS, CHIP_COLS)
        term = dot(left, dbuf[c].reshape(2 * ROWS, KVW), ((0,), (0,)))
        if first:
            acc[...] = term
        else:
            acc[...] += term

    for c in range(0, 4):
        row_grad(c)
    back.first_near(0)
    back.first_near(1)
    for c in range(4, 8):
        row_grad(c)
    back.second_near(0, 0)
    back.second_near(1, 0)
    back.first_far(0)
    back.first_far(1)
    for c in range(8, 12):
        row_grad(c)
    grad(chip, True)
    for j in (1, 2):
        back.second_near(0, j)
        back.second_near(1, j)
    for c in range(12, 16):
        row_grad(c)
    for dx, dy in ((1, 0), (-1, 0), (0, 1), (0, -1)):
        grad(chip_at(dx, dy))
    back.second_near(0, 3)
    back.second_near(1, 3)
    dh_copy = row_out()
    for dx, dy in ((1, 1), (-1, 1), (1, -1), (-1, -1)):
        grad(chip_at(dx, dy))
    back.second_far(0, 0)
    back.second_far(1, 0)
    for dx, dy in ((2, 0), (0, 2)):
        grad(chip_at(dx, dy))
    for j in (1, 2):
        back.second_far(0, j)
        back.second_far(1, j)
    for dx, dy in ((2, 1), (2, -1), (1, 2), (-1, 2)):
        grad(chip_at(dx, dy))
    back.second_far(0, 3)
    back.second_far(1, 3)
    grad(chip_at(2, 2))

    grad_scale = 1.0 / math.sqrt(ROWS * 2 * CHIPS * ROLL)
    ps[...] = (acc[...] * grad_scale).astype(BF16).reshape(ROLL, SLICE, KVW)
    last = []
    for d in range(1, ROLL):
        to = lax.rem(z + d, ROLL)
        copy = pltpu.make_async_remote_copy(
            src_ref=ps.at[to], dst_ref=rs.at[z],
            send_sem=r_send.at[d], recv_sem=r_recv.at[d],
            device_id={"roll": to}, device_id_type=MESH,
        )
        copy.start()
        last.append(copy)
    rs[z] = ps[z]
    for d in range(1, ROLL):
        ref = rs.at[lax.rem(z + ROLL - d, ROLL)]
        pltpu.make_async_copy(ref, ref, r_recv.at[d]).wait()
    total = rs[0].astype(F32)
    for s in range(1, ROLL):
        total = total + rs[s].astype(F32)
    rd[...] = total.astype(BF16)
    owner = z // (ROLL // 2)
    place = lax.rem(z, ROLL // 2)

    def hand_over(to, d):
        return pltpu.make_async_remote_copy(
            src_ref=rd, dst_ref=og.at[core, place],
            send_sem=o_send.at[d], recv_sem=o_recv.at[core, place],
            device_id={"roll": to, "fsdp": chip * 2 + owner}, device_id_type=MESH,
        )

    for d in range(1, ROLL):
        copy = hand_over(lax.rem(z + d, ROLL), d)
        copy.start()
        last.append(copy)

    @pl.when(owner != core)
    def _():
        hand_over(z, 0).start()

    @pl.when(owner == core)
    def _():
        og[core, place] = rd[...]

    for s in range(ROLL // 2):
        for k in range(2):
            ref = og.at[k, s]
            own = (core * (ROLL // 2) + s == z) & (core == k)

            @pl.when(jnp.logical_not(own))
            def _():
                pltpu.make_async_copy(ref, ref, o_recv.at[k, s]).wait()

    for k in range(2):
        kgv[:, k * KVW:(k + 1) * KVW] = og[k].astype(F32).reshape(ROWS, KVW)
    kg_copy = local(kgv, kg_out, 10)

    @pl.when(owner != core)
    def _():
        hand_over(z, 0).wait_send()

    gather.finish()
    back.finish()
    for copy in pair_copies + n_copies + z_copies + last:
        copy.wait_send()
    for copy in dq_copies:
        copy.wait()
    dh_copy.wait()
    kg_copy.wait()


def shards(
    hidden, send_counts, queries, upstream, norm_gain, kv_weight,
    logp_new, logp_old, advantage, segment_ids, trim_mask,
):
    anywhere = pl.BlockSpec(memory_space=pl.ANY)
    vmem = pl.BlockSpec(memory_space=pltpu.VMEM)
    smem = pl.BlockSpec(memory_space=pltpu.SMEM)
    dma = pltpu.SemaphoreType.DMA
    relay_buf = pltpu.VMEM((KV, ROLL, 2 * SLOT, HD), BF16)
    rows = pltpu.VMEM((ROWS, D), BF16)
    return pl.pallas_call(
        body,
        out_shape=(
            jax.ShapeDtypeStruct((ROWS, D), BF16),
            jax.ShapeDtypeStruct((ROWS, D), BF16),
            jax.ShapeDtypeStruct((ROWS, 2 * KVW), F32),
        ),
        in_specs=[anywhere, smem, anywhere, anywhere, vmem, anywhere, vmem, vmem, smem, vmem, vmem],
        out_specs=(anywhere, anywhere, anywhere),
        scratch_shapes=[
            rows, rows, rows, rows, rows,
            pltpu.VMEM((2, ROWS, D), BF16),
            pltpu.VMEM((ROWS, D), F32),
            pltpu.VMEM((CHIPS, 2, ROWS, KVW), BF16),
            pltpu.VMEM((CHIPS, 2, ROWS, KVW), BF16),
            pltpu.VMEM((CHIPS, 2, ROWS, KVW), BF16),
            pltpu.VMEM((CHIPS, 2, ROWS, CHIP_COLS), BF16),
            pltpu.VMEM((2 * ROWS, KVW), F32),
            pltpu.VMEM((2, ROWS, KVW), BF16),
            pltpu.VMEM((2, ROWS, KVW), BF16),
            pltpu.VMEM((2, ROWS, KVW), BF16),
            pltpu.VMEM((PACKED, 2 * ROWS), BF16),
            pltpu.VMEM((PACKED, 2 * ROWS), BF16),
            pltpu.VMEM((2 * ROWS, PACKED), BF16),
            pltpu.VMEM((2 * ROWS, PACKED), BF16),
            relay_buf, relay_buf, relay_buf, relay_buf,
            pltpu.VMEM((ROWS, HD), F32),
            pltpu.VMEM((ROWS, ROWS), F32),
            pltpu.VMEM((ROWS, ROWS), F32),
            pltpu.VMEM((ROLL, SLICE, KVW), BF16),
            pltpu.VMEM((ROLL, SLICE, KVW), BF16),
            pltpu.VMEM((SLICE, KVW), BF16),
            pltpu.VMEM((2, ROLL // 2, SLICE, KVW), BF16),
            pltpu.VMEM((ROWS, 2 * KVW), F32),
            dma((11,)), dma((6,)), dma((6,)),
            dma((40,)), dma((2, 20)), dma((40,)), dma((2, 20)),
            dma((CHIPS,)), dma((CHIPS,)),
            dma((KV, ROLL)), dma((KV, ROLL)), dma((KV, ROLL)), dma((KV, ROLL)),
            dma((ROLL,)), dma((ROLL,)), dma((ROLL,)), dma((2, ROLL // 2)),
        ],
        compiler_params=pltpu.CompilerParams(
            collective_id=0, has_side_effects=True, vmem_limit_bytes=60 << 20
        ),
        name="backward",
    )(
        hidden, send_counts, queries, upstream, norm_gain.reshape(1, D), kv_weight,
        logp_new, logp_old, advantage, segment_ids, trim_mask,
    )


def solution(mesh):
    placed = (
        P(("roll", "fsdp"), None),
        P("fsdp", None, None),
        P(("roll", "fsdp"), None),
        P(("roll", "fsdp"), None),
        P(),
        P("fsdp", None),
        P(("roll", "fsdp"), None),
        P(("roll", "fsdp"), None),
        P(("roll", "fsdp"), None),
        P(("roll", "fsdp"), None),
        P(("roll", "fsdp"), None),
    )
    return jax.shard_map(
        shards,
        mesh=mesh,
        in_specs=placed,
        out_specs=(P(("roll", "fsdp"), None), P(("roll", "fsdp"), None), P("fsdp", None)),
        check_vma=False,
    )
```

time: 301 us -> 112 us (0.37); the launches traced: 297 us -> 112 us
  waiting for transfers between devices: 189 us -> 0 us
  Pallas kernels: 0 us -> 107 us
  matrix products: 28.9 us -> 0 us
  other arithmetic: 27.1 us -> 0 us
  local copies, waits for them, and re-layouts: 21.4 us -> 4.57 us
  starting transfers between devices: 16.1 us -> 0 us
  between operations: 14.1 us -> 0.65 us
    pallas_call x0 -> x1, Pallas kernels: none -> 107 us  [shards(): pl.pallas_call(body, out_shape=(jax.ShapeDtypeStruct((ROWS, D), BF16), ja...]
    psum x1 -> x0, waiting for transfers between devices: 69.4 us -> none  [shards(): summed = lax.psum(share, 'roll')]
    reduce_scatter x1 -> x0, waiting for transfers between devices: 58.7 us -> none  [shards(): lax.psum_scatter(lax.dot_general(normed, d_kv, (((0,), (0,)), ((), ())),...]
    all_to_all x2 -> x0, waiting for transfers between devices: 52.1 us -> none  [the longest x1 27.3 us: shards(): lax.all_to_all(pack_rows(d_rows, recv_starts, slot_cap), 'roll', split_ax...]
    dot_general x8 -> x0, matrix products: 26.1 us -> none  [the longest x1 8.2 us: shards(): lax.dot_general(normed, d_kv, (((0,), (0,)), ((), ())), preferred_element...]
    all_to_all x2 -> x0, starting transfers between devices: 16 us -> none  [the longest x1 9.16 us: shards(): lax.all_to_all(pack_rows(hidden, send_starts, slot_cap), 'roll', split_ax...]
    and x5 -> x0, other arithmetic: 10.7 us -> none  [the longest x2 10.1 us: unpack_rows(): jnp.take(buffer.reshape(peer_count * slot_cap, row_width), flat_index, ax...]
    gather x6 -> x0, local copies, waits for them, and re-layouts: 10.2 us -> none  [the longest x2 4.47 us: pack_rows(): chosen = jnp.take(source_rows, picks.reshape(-1), axis=0)]
  transfers between devices with their start and end apart: 5 -> 0, of which waited for: 5 -> 0; matrix products, arithmetic and copies ran while one was open for 17% -> 0% of each run, Pallas kernels for 0% -> 0%
where the time goes in v2:
time: 112 us
  Pallas kernels  107 us (96%)
  local copies, waits for them, and re-layouts  4.57 us (4%)
    pallas_call x1, Pallas kernels, shards(): pl.pallas_call(body, out_shape=(jax.ShapeDtypeStruct((ROWS, D), BF16), ja...  107 us
    unnamed x7, local copies, waits for them, and re-layouts  4.57 us

profile of v2, /device:TPU:1, one launch (start us, length us, event | category | flops | bytes accessed | tf_op | source)
XLA Modules:
  0.0 111.7 jit_solution(17918119082179541945)
XLA Ops:
  0.6 106.5 %backward.1 = (bf16[128,4096]{1,0:T(8,128)(2,1)}, bf16[128,4096]{1,0:T(8,128)(2,1)}, f32[128,1024]{1,0:T(8,128)}) custom-call(bf16[128,4096]{1,0:T(8,128)(2,1)} %hid.1, s32[1,8,8]{2,1,0:T(8,128)} %cnt.1, bf16[128,4096]{1,0:T(8,128)(2,1)} %qry.1, bf16[128,4096]{1,0:T(8,128)(2,1)} %ups.1, f32[1,4096]{1,0:T(1,128)} %bitcast.1, bf16[128,1024]{1,0:T(8,128)(2,1)} %wgt.1, ...), custom_call_target="tpu_custom_call" | custom-call | tf_op jit(solution)/shard_map/backward/pallas_call | solution.py:537
  107.2 0.0 copy-start
  107.2 2.4 %copy.17 = bf16[128,4096]{1,0:T(8,128)(2,1)} copy(bf16[128,4096]{1,0:T(8,128)(2,1)} %get-tuple-element.6) | data formatting | bytes 2097152
  109.6 0.0 copy-done
  109.6 0.0 copy-start.1
  109.6 1.0 copy.18
  110.5 0.4 copy-done.1
  111.0 0.8 copy.19
Async XLA Ops:
  107.2 2.4 %copy-start = (bf16[128,4096]{1,0:T(8,128)(2,1)S(1)}, bf16[128,4096]{1,0:T(8,128)(2,1)}, u32[]{:S(2)}) copy-start(bf16[128,4096]{1,0:T(8,128)(2,1)} %get-tuple-element.7) | copy-start | bytes 3145732
  109.6 1.4 %copy-start.1 = (f32[128,1024]{1,0:T(8,128)S(1)}, f32[128,1024]{1,0:T(8,128)}, u32[]{:S(2)}) copy-start(f32[128,1024]{1,0:T(8,128)} %get-tuple-element.8) | copy-start | bytes 1572868

commit v3 on v2

--- a/solution.py
+++ b/solution.py
@@ -21,7 +21,9 @@
 PACKED = ROLL * 2 * SLOT
 CHIP_COLS = D // CHIPS
 SLICE = 2 * ROWS // ROLL
-CHUNKS = 1
+D_CHUNKS = 2
+WIDTH = KVW // D_CHUNKS
+PIECES = 4
 
 ratio_cap = 2.0
 norm_eps = 1e-06
@@ -35,7 +37,8 @@
 
 
 class Gather:
-    def __init__(self, buf, send_sem, recv_sem, x, y, core):
+    def __init__(self, buf, send_sem, recv_sem, x, y, core, cols=slice(0, KVW)):
+        self.cols = pl.ds(cols.start, cols.stop - cols.start)
         self.buf, self.send_sem, self.recv_sem = buf, send_sem, recv_sem
         self.x, self.y, self.core = x, y, core
         self.started = []
@@ -46,8 +49,8 @@
         return chip * 2 + self.core, chip
 
     def view(self, half, du, dv, quarter):
-        ref = self.buf.at[self.at(half, du, dv)[1], half]
-        return ref if quarter is None else ref.at[pl.ds(quarter * (ROWS // 2), ROWS // 2)]
+        rows = pl.ds(0, ROWS) if quarter is None else pl.ds(quarter * (ROWS // 2), ROWS // 2)
+        return self.buf.at[self.at(half, du, dv)[1], half, rows, self.cols]
 
     def send(self, half, block, step, sem, quarter=None):
         n = len(self.started)
@@ -331,7 +334,7 @@
     u_copy.wait()
     scale = 1.0 / math.sqrt(HD)
     stacked = (GROUP, ROWS, ROWS)
-    dq_copies = []
+    out_copies = []
     for h in range(KV):
         relayed(rv, z_recv, h)
         kv = dot(unpack_r[...], rv[h].reshape(PACKED, HD)).astype(BF16)
@@ -362,28 +365,46 @@
         d_q = dot(d_scores, keys).astype(BF16)
         for g in range(GROUP):
             dqv[:, base + g * HD:base + (g + 1) * HD] = d_q[g * ROWS:(g + 1) * ROWS]
-        dq_copies.append(
+        out_copies.append(
             local(dqv.at[:, pl.ds(base, GROUP * HD)], dq_out.at[:, pl.ds(base, GROUP * HD)], 5 + h)
         )
 
-    for d in range(1, CHIPS):
-        ref = ncols.at[lax.rem(chip + CHIPS - d, CHIPS), core]
-        pltpu.make_async_copy(ref, ref, n_recv.at[d]).wait()
-    n_own.wait()
-    to_partner(ncols.at[:, core], ncols.at[:, core], 4)
-
-    for h in range(KV):
+    def span(g):
+        return slice(g * WIDTH, (g + 1) * WIDTH)
+
+    def returned(h):
         relayed(rv2, b_recv, h)
         back = dot(unpack_s[...], rv2[h].reshape(PACKED, HD)).astype(BF16)
         cols = slice(h * HD, (h + 1) * HD)
         dkvown[0, :, cols] = back[:ROWS]
         dkvown[1, :, cols] = back[ROWS:]
-    to_partner(dkvown.at[other], dbuf.at[chip, core], 5)
-    dbuf[chip, core] = dkvown[core]
-    from_partner(dbuf.at[chip, other], 5)
-    back = Gather(dbuf, d_send, d_recv, x, y, core)
-    by_owner(back.own)
-    from_partner(ncols.at[:, other], 4)
+
+    def exchange(g):
+        ds = pl.ds(g * WIDTH, WIDTH)
+        to_partner(dkvown.at[other, :, ds], dbuf.at[chip, core, :, ds], 5 + g)
+        dbuf[chip, core, :, span(g)] = dkvown[core, :, span(g)]
+
+    backs = [
+        Gather(dbuf, d_send.at[g], d_recv.at[g], x, y, core, span(g)) for g in range(D_CHUNKS)
+    ]
+
+    def begin(g):
+        from_partner(dbuf.at[chip, other, :, pl.ds(g * WIDTH, WIDTH)], 5 + g)
+        by_owner(backs[g].own)
+
+    returned(0)
+    returned(1)
+    exchange(0)
+    returned(2)
+    begin(0)
+    returned(3)
+    exchange(1)
+    for d in range(1, CHIPS):
+        ref = ncols.at[lax.rem(chip + CHIPS - d, CHIPS), core]
+        pltpu.make_async_copy(ref, ref, n_recv.at[d]).wait()
+    n_own.wait()
+    begin(1)
+    to_partner(ncols.at[:, core], ncols.at[:, core], 4)
     from_partner(wother, 3)
 
     moment = [jnp.zeros((ROWS, HD), F32)]
@@ -406,122 +427,170 @@
             cols = slice(c * CHIP_COLS, (c + 1) * CHIP_COLS)
             unit = hv[:, cols].astype(F32) * inv_rms
             dhv[:, cols] = (inv_rms * (dn[:, cols] - unit * mean)).astype(BF16)
-        return local(dhv, dh_out, 9)
-
-    def grad(c, first=False):
-        left = ncols[c].reshape(2 * ROWS, CHIP_COLS)
-        term = dot(left, dbuf[c].reshape(2 * ROWS, KVW), ((0,), (0,)))
-        if first:
-            acc[...] = term
+        out_copies.append(local(dhv, dh_out, 9))
+
+    def grad(g, *offsets):
+        cols = span(g)
+        term = None
+        for dx, dy in offsets:
+            c = chip_at(dx, dy)
+            left = ncols[c].reshape(2 * ROWS, CHIP_COLS)
+            part = dot(left, dbuf[c, :, :, cols].reshape(2 * ROWS, WIDTH), ((0,), (0,)))
+            term = part if term is None else term + part
+        if (0, 0) in offsets:
+            acc[:, cols] = term
         else:
-            acc[...] += term
-
-    for c in range(0, 4):
-        row_grad(c)
-    back.first_near(0)
-    back.first_near(1)
-    for c in range(4, 8):
-        row_grad(c)
-    back.second_near(0, 0)
-    back.second_near(1, 0)
-    back.first_far(0)
-    back.first_far(1)
-    for c in range(8, 12):
-        row_grad(c)
-    grad(chip, True)
-    for j in (1, 2):
-        back.second_near(0, j)
-        back.second_near(1, j)
-    for c in range(12, 16):
-        row_grad(c)
-    for dx, dy in ((1, 0), (-1, 0), (0, 1), (0, -1)):
-        grad(chip_at(dx, dy))
-    back.second_near(0, 3)
-    back.second_near(1, 3)
-    dh_copy = row_out()
-    for dx, dy in ((1, 1), (-1, 1), (1, -1), (-1, -1)):
-        grad(chip_at(dx, dy))
-    back.second_far(0, 0)
-    back.second_far(1, 0)
-    for dx, dy in ((2, 0), (0, 2)):
-        grad(chip_at(dx, dy))
-    for j in (1, 2):
-        back.second_far(0, j)
-        back.second_far(1, j)
-    for dx, dy in ((2, 1), (2, -1), (1, 2), (-1, 2)):
-        grad(chip_at(dx, dy))
-    back.second_far(0, 3)
-    back.second_far(1, 3)
-    grad(chip_at(2, 2))
+            acc[:, cols] += term
+
+    near = ((1, 0), (-1, 0), (0, 1), (0, -1))
+    corners = ((1, 1), (-1, 1), (1, -1), (-1, -1))
+    knights = ((2, 1), (2, -1), (1, 2), (-1, 2))
+
+    def both(do, *args):
+        do(0, *args)
+        do(1, *args)
 
     grad_scale = 1.0 / math.sqrt(ROWS * 2 * CHIPS * ROLL)
-    ps[...] = (acc[...] * grad_scale).astype(BF16).reshape(ROLL, SLICE, KVW)
-    last = []
-    for d in range(1, ROLL):
-        to = lax.rem(z + d, ROLL)
-        copy = pltpu.make_async_remote_copy(
-            src_ref=ps.at[to], dst_ref=rs.at[z],
-            send_sem=r_send.at[d], recv_sem=r_recv.at[d],
-            device_id={"roll": to}, device_id_type=MESH,
-        )
-        copy.start()
-        last.append(copy)
-    rs[z] = ps[z]
-    for d in range(1, ROLL):
-        ref = rs.at[lax.rem(z + ROLL - d, ROLL)]
-        pltpu.make_async_copy(ref, ref, r_recv.at[d]).wait()
-    total = rs[0].astype(F32)
-    for s in range(1, ROLL):
-        total = total + rs[s].astype(F32)
-    rd[...] = total.astype(BF16)
     owner = z // (ROLL // 2)
     place = lax.rem(z, ROLL // 2)
-
-    def hand_over(to, d):
+    last = []
+
+    def scatter(g):
+        cols, ds = span(g), pl.ds(g * WIDTH, WIDTH)
+        ps[:, :, cols] = (acc[:, cols] * grad_scale).astype(BF16).reshape(ROLL, SLICE, WIDTH)
+        for d in range(1, ROLL):
+            to = lax.rem(z + d, ROLL)
+            copy = pltpu.make_async_remote_copy(
+                src_ref=ps.at[to, :, ds], dst_ref=rs.at[z, :, ds],
+                send_sem=r_send.at[g, d], recv_sem=r_recv.at[g, d],
+                device_id={"roll": to}, device_id_type=MESH,
+            )
+            copy.start()
+            last.append(copy)
+        rs[z, :, cols] = ps[z, :, cols]
+
+    def hand_over(to, d, g):
+        ds = pl.ds(g * WIDTH, WIDTH)
         return pltpu.make_async_remote_copy(
-            src_ref=rd, dst_ref=og.at[core, place],
-            send_sem=o_send.at[d], recv_sem=o_recv.at[core, place],
+            src_ref=rd.at[:, ds], dst_ref=og.at[core, place, :, ds],
+            send_sem=o_send.at[g, d], recv_sem=o_recv.at[g, core, place],
             device_id={"roll": to, "fsdp": chip * 2 + owner}, device_id_type=MESH,
         )
 
-    for d in range(1, ROLL):
-        copy = hand_over(lax.rem(z + d, ROLL), d)
-        copy.start()
-        last.append(copy)
+    def reduce(g):
+        cols, ds = span(g), pl.ds(g * WIDTH, WIDTH)
+        for d in range(1, ROLL):
+            ref = rs.at[lax.rem(z + ROLL - d, ROLL), :, ds]
+            pltpu.make_async_copy(ref, ref, r_recv.at[g, d]).wait()
+        total = rs[0, :, cols].astype(F32)
+        for s in range(1, ROLL):
+            total = total + rs[s, :, cols].astype(F32)
+        rd[:, cols] = total.astype(BF16)
+        for d in range(1, ROLL):
+            copy = hand_over(lax.rem(z + d, ROLL), d, g)
+            copy.start()
+            last.append(copy)
+
+        @pl.when(owner != core)
+        def _():
+            hand_over(z, 0, g).start()
+
+        @pl.when(owner == core)
+        def _():
+            og[core, place, :, cols] = rd[:, cols]
+
+    def collect(g):
+        cols, ds = span(g), pl.ds(g * WIDTH, WIDTH)
+        for s in range(ROLL // 2):
+            for k in range(2):
+                ref = og.at[k, s, :, ds]
+                own = (core * (ROLL // 2) + s == z) & (core == k)
+
+                @pl.when(jnp.logical_not(own))
+                def _():
+                    pltpu.make_async_copy(ref, ref, o_recv.at[g, k, s]).wait()
+
+        for k in range(2):
+            out = slice(k * KVW + cols.start, k * KVW + cols.stop)
+            kgv[:, out] = og[k, :, :, cols].astype(F32).reshape(ROWS, WIDTH)
+
+    first, second = backs
+    both(first.first_near)
+    for c in range(0, 3):
+        row_grad(c)
+    both(first.second_near, 0)
+    both(first.first_far)
+    both(second.first_near)
+    for c in range(3, 6):
+        row_grad(c)
+    both(first.second_near, 1)
+    both(first.second_near, 2)
+    both(second.second_near, 0)
+    both(second.first_far)
+    from_partner(ncols.at[:, other], 4)
+    grad(0, (0, 0), *near)
+    both(first.second_near, 3)
+    both(second.second_near, 1)
+    both(second.second_near, 2)
+    grad(0, *corners)
+    both(first.second_far, 0)
+    grad(0, (2, 0), (0, 2))
+    both(first.second_far, 1)
+    both(first.second_far, 2)
+    grad(0, *knights)
+    both(first.second_far, 3)
+    grad(0, (2, 2))
+    scatter(0)
+    both(second.second_near, 3)
+    for c in range(6, 16):
+        row_grad(c)
+    grad(1, (0, 0), *near, *corners)
+    row_out()
+    both(second.second_far, 0)
+    grad(1, (2, 0), (0, 2))
+    both(second.second_far, 1)
+    both(second.second_far, 2)
+    grad(1, *knights)
+    both(second.second_far, 3)
+    grad(1, (2, 2))
+    scatter(1)
+    reduce(0)
+    reduce(1)
+    collect(0)
+    collect(1)
+    out_copies.append(local(kgv, kg_out, 10))
 
     @pl.when(owner != core)
     def _():
-        hand_over(z, 0).start()
-
-    @pl.when(owner == core)
-    def _():
-        og[core, place] = rd[...]
-
-    for s in range(ROLL // 2):
-        for k in range(2):
-            ref = og.at[k, s]
-            own = (core * (ROLL // 2) + s == z) & (core == k)
-
-            @pl.when(jnp.logical_not(own))
-            def _():
-                pltpu.make_async_copy(ref, ref, o_recv.at[k, s]).wait()
-
-    for k in range(2):
-        kgv[:, k * KVW:(k + 1) * KVW] = og[k].astype(F32).reshape(ROWS, KVW)
-    kg_copy = local(kgv, kg_out, 10)
-
-    @pl.when(owner != core)
-    def _():
-        hand_over(z, 0).wait_send()
+        for g in range(D_CHUNKS):
+            hand_over(z, 0, g).wait_send()
 
     gather.finish()
-    back.finish()
+    for back in backs:
+        back.finish()
     for copy in pair_copies + n_copies + z_copies + last:
         copy.wait_send()
-    for copy in dq_copies:
+    for copy in out_copies:
         copy.wait()
-    dh_copy.wait()
-    kg_copy.wait()
+
+
+def store(*refs):
+    sources, outs, buffers, (in_sem, out_sem) = refs[:3], refs[3:6], refs[6:9], refs[9:]
+    arrivals, leaving = [], []
+    rows = ROWS // PIECES
+    for piece in range(PIECES):
+        part = pl.ds(piece * rows, rows)
+        for n in range(3):
+            copy = pltpu.make_async_copy(sources[n].at[part], buffers[n].at[part], in_sem.at[n, piece])
+            copy.start()
+            arrivals.append((copy, n, piece, part))
+    for copy, n, piece, part in arrivals:
+        copy.wait()
+        out = pltpu.make_async_copy(buffers[n].at[part], outs[n].at[part], out_sem.at[n, piece])
+        out.start()
+        leaving.append(out)
+    for out in leaving:
+        out.wait()
 
 
 def shards(
@@ -534,7 +603,7 @@
     dma = pltpu.SemaphoreType.DMA
     relay_buf = pltpu.VMEM((KV, ROLL, 2 * SLOT, HD), BF16)
     rows = pltpu.VMEM((ROWS, D), BF16)
-    return pl.pallas_call(
+    results = pl.pallas_call(
         body,
         out_shape=(
             jax.ShapeDtypeStruct((ROWS, D), BF16),
@@ -568,11 +637,11 @@
             pltpu.VMEM((SLICE, KVW), BF16),
             pltpu.VMEM((2, ROLL // 2, SLICE, KVW), BF16),
             pltpu.VMEM((ROWS, 2 * KVW), F32),
-            dma((11,)), dma((6,)), dma((6,)),
-            dma((40,)), dma((2, 20)), dma((40,)), dma((2, 20)),
+            dma((11,)), dma((7,)), dma((7,)),
+            dma((40,)), dma((2, 20)), dma((D_CHUNKS, 40)), dma((D_CHUNKS, 2, 20)),
             dma((CHIPS,)), dma((CHIPS,)),
             dma((KV, ROLL)), dma((KV, ROLL)), dma((KV, ROLL)), dma((KV, ROLL)),
-            dma((ROLL,)), dma((ROLL,)), dma((ROLL,)), dma((2, ROLL // 2)),
+            dma((D_CHUNKS, ROLL)), dma((D_CHUNKS, ROLL)), dma((D_CHUNKS, ROLL)), dma((D_CHUNKS, 2, ROLL // 2)),
         ],
         compiler_params=pltpu.CompilerParams(
             collective_id=0, has_side_effects=True, vmem_limit_bytes=60 << 20
@@ -582,6 +651,15 @@
         hidden, send_counts, queries, upstream, norm_gain.reshape(1, D), kv_weight,
         logp_new, logp_old, advantage, segment_ids, trim_mask,
     )
+    return pl.pallas_call(
+        store,
+        out_shape=tuple(jax.ShapeDtypeStruct(a.shape, a.dtype) for a in results),
+        in_specs=[anywhere] * 3,
+        out_specs=(anywhere,) * 3,
+        scratch_shapes=[pltpu.VMEM(a.shape, a.dtype) for a in results] + [dma((3, PIECES)), dma((3, PIECES))],
+        compiler_params=pltpu.CompilerParams(vmem_limit_bytes=60 << 20),
+        name="store",
+    )(*results)
 
 
 def solution(mesh):

time: 112 us -> 107 us (0.955)
  local copies, waits for them, and re-layouts: 4.57 us -> 0 us
    unnamed x7 -> x0, local copies, waits for them, and re-layouts: 4.57 us -> none
    pallas_call x1, Pallas kernels: 107 us -> 103 us  [shards(): pl.pallas_call(body, out_shape=(jax.ShapeDtypeStruct((ROWS, D), BF16), ja...]
    pallas_call x0 -> x1, Pallas kernels: none -> 2.63 us  [shards(): pl.pallas_call(store, out_shape=tuple((jax.ShapeDtypeStruct(a.shape, a.dt...]
where the time goes in v3:
time: 107 us
  Pallas kernels  106 us (99%)
    pallas_call x1, Pallas kernels, shards(): pl.pallas_call(body, out_shape=(jax.ShapeDtypeStruct((ROWS, D), BF16), ja...  103 us
    pallas_call x1, Pallas kernels, shards(): pl.pallas_call(store, out_shape=tuple((jax.ShapeDtypeStruct(a.shape, a.dt...  2.63 us

profile of v3, /device:TPU:1, one launch (start us, length us, event | category | flops | bytes accessed | tf_op | source)
XLA Modules:
  0.0 106.7 jit_solution(14673004855593280028)
XLA Ops:
  0.6 103.5 %backward.1 = (bf16[128,4096]{1,0:T(8,128)(2,1)}, bf16[128,4096]{1,0:T(8,128)(2,1)}, f32[128,1024]{1,0:T(8,128)}) custom-call(bf16[128,4096]{1,0:T(8,128)(2,1)} %hid.1, s32[1,8,8]{2,1,0:T(8,128)} %cnt.1, bf16[128,4096]{1,0:T(8,128)(2,1)} %qry.1, bf16[128,4096]{1,0:T(8,128)(2,1)} %ups.1, f32[1,4096]{1,0:T(1,128)} %bitcast.1, bf16[128,1024]{1,0:T(8,128)(2,1)} %wgt.1, ...), custom_call_target="tpu_custom_call" | custom-call | tf_op jit(solution)/shard_map/backward/pallas_call | solution.py:606
  104.1 2.6 %store.1 = (bf16[128,4096]{1,0:T(8,128)(2,1)}, bf16[128,4096]{1,0:T(8,128)(2,1)}, f32[128,1024]{1,0:T(8,128)}) custom-call(bf16[128,4096]{1,0:T(8,128)(2,1)} %get-tuple-element.6.refs_0_, bf16[128,4096]{1,0:T(8,128)(2,1)} %get-tuple-element.7.refs_1_, f32[128,1024]{1,0:T(8,128)} %get-tuple-element.8.refs_2_), custom_call_target="tpu_custom_call" | custom-call | tf_op jit(solution)/shard_map/store/pallas_call | solution.py:654

commit v4 on v3

--- a/solution.py
+++ b/solution.py
@@ -293,13 +293,6 @@
         kvx[r] = acc[r * ROWS:(r + 1) * ROWS, :].astype(BF16)
     to_partner(kvx.at[other], kvown.at[core], 2)
     kvown[core] = kvx[core]
-    to_partner(wbuf, wother, 3)
-    for copy in n_copies:
-        copy.start()
-    n_own = local(
-        nb.at[core, :, pl.ds(pl.multiple_of(chip * CHIP_COLS, CHIP_COLS), CHIP_COLS)],
-        ncols.at[chip, core], 4,
-    )
     from_partner(kvown.at[other], 2)
 
     def heads(ref, h):
@@ -330,6 +323,13 @@
         pk[h] = packed.reshape(ROLL, 2 * SLOT, HD)
         relay(pk, rv, z_send, z_recv, h)
 
+    to_partner(wbuf, wother, 3)
+    for copy in n_copies:
+        copy.start()
+    n_own = local(
+        nb.at[core, :, pl.ds(pl.multiple_of(chip * CHIP_COLS, CHIP_COLS), CHIP_COLS)],
+        ncols.at[chip, core], 4,
+    )
     q_copy.wait()
     u_copy.wait()
     scale = 1.0 / math.sqrt(HD)

time: 107 us -> 106 us (level)
  no operation moved by 1% of the time
where the time goes in v4:
time: 106 us
  Pallas kernels  105 us (99%)
    pallas_call x1, Pallas kernels, shards(): pl.pallas_call(body, out_shape=(jax.ShapeDtypeStruct((ROWS, D), BF16), ja...  103 us
    pallas_call x1, Pallas kernels, shards(): pl.pallas_call(store, out_shape=tuple((jax.ShapeDtypeStruct(a.shape, a.dt...  2.63 us

profile of v4, /device:TPU:1, one launch (start us, length us, event | category | flops | bytes accessed | tf_op | source)
XLA Modules:
  0.0 106.3 jit_solution(2005844017013977336)
XLA Ops:
  0.6 102.9 %backward.1 = (bf16[128,4096]{1,0:T(8,128)(2,1)}, bf16[128,4096]{1,0:T(8,128)(2,1)}, f32[128,1024]{1,0:T(8,128)}) custom-call(bf16[128,4096]{1,0:T(8,128)(2,1)} %hid.1, s32[1,8,8]{2,1,0:T(8,128)} %cnt.1, bf16[128,4096]{1,0:T(8,128)(2,1)} %qry.1, bf16[128,4096]{1,0:T(8,128)(2,1)} %ups.1, f32[1,4096]{1,0:T(1,128)} %bitcast.1, bf16[128,1024]{1,0:T(8,128)(2,1)} %wgt.1, ...), custom_call_target="tpu_custom_call" | custom-call | tf_op jit(solution)/shard_map/backward/pallas_call | solution.py:606
  103.5 2.6 %store.1 = (bf16[128,4096]{1,0:T(8,128)(2,1)}, bf16[128,4096]{1,0:T(8,128)(2,1)}, f32[128,1024]{1,0:T(8,128)}) custom-call(bf16[128,4096]{1,0:T(8,128)(2,1)} %get-tuple-element.6.refs_0_, bf16[128,4096]{1,0:T(8,128)(2,1)} %get-tuple-element.7.refs_1_, f32[128,1024]{1,0:T(8,128)} %get-tuple-element.8.refs_2_), custom_call_target="tpu_custom_call" | custom-call | tf_op jit(solution)/shard_map/store/pallas_call | solution.py:654
